TPU v7x, 32 devices: a whole 2x2x4 slice. The times are simulated.
32 devices in a mesh: vol: 8 (over z, x), nar: 4 (over y, core).
Axes of the slice: x: 2, y: 2, z: 4, core: 2. Of those that a mesh axis runs over, the one named last changes fastest.
Arguments:
- series: bfloat16 [2048, 2048], P(('vol', 'nar')), may hold values from -6 to 6
- send_rows: int32 [8, 4, 16], P('vol', 'nar'), may hold values from -1 to 63, as said below
- bin_counts: int32 [4], replicated, may hold values from 1 to 128, 256 in all
- observer_cells: int32 [2, 512], replicated, may hold values from 0 to 127
Outputs:
- spectra_out: float32 [4, 128, 2, 512], P('nar', 'vol')
Inputs may be any that keep to these rules, and one draw needn't show every extreme that they name: `send_rows`: entry (u, n, k) names the row of device (u, n)'s 64 rows of series for slot k mod 2 bound for the patch owner at vol index k // 2 and nar index n, or is -1 for an empty slot; one device never names a row twice. Nar index m owns bin_counts[m] bins in order, from the sum of the counts before m on; some owner holds exactly 128 bins. `observer_cells`: row 0 holds polar indices, row 1 azimuthal indices.
All inputs are finite; a program needn't handle non-finite values.
Results may differ from a plain program's by a relative error of at most 0.0043.
Values may be sent and summed in bfloat16 or wider, within the bound.
No kernel may reach another device: no remote copies, remote signals or barrier semaphores. Data moves between devices by JAX's collectives and lax.ppermute only.
A program may use at most 64 MiB of HBM per device.

v0:
```python
import math

import jax
import jax.numpy as jnp
from jax import lax
from jax.sharding import PartitionSpec as P

NF = 256
NQ = 4


WAVE_STEP = 0.05


def dft_table(bin_ids, keep_bin, time_len):
    time_steps = jnp.arange(time_len, dtype=jnp.int32)
    frequency = bin_ids + 1
    phase_turns = time_steps[:, None] * frequency[None, :] % time_len
    angle_grid = phase_turns.astype(jnp.float32) * (2.0 * math.pi / time_len)
    dft_grid = jnp.stack([jnp.cos(angle_grid), -jnp.sin(angle_grid)], axis=-1)
    dft_grid = jnp.where(keep_bin[None, :, None], dft_grid, jnp.float32(0.0))
    return dft_grid.reshape(time_len, 2 * bin_ids.shape[0]).astype(jnp.bfloat16)


def positions(point_list):
    beside_all = (point_list * 1597 % 8191).astype(jnp.float32) * (2.0 * math.pi / 8191.0)
    jitter = (point_list * 613 % 127).astype(jnp.float32) * (0.37 / 127.0)
    axial = (point_list // 128).astype(jnp.float32) * 0.5 + jitter
    return (20.0 * jnp.cos(beside_all), 20.0 * jnp.sin(beside_all), axial)


def directions(obs_cells):
    polar_angle = (obs_cells[0].astype(jnp.float32) + 0.5) * (math.pi / 128.0)
    azimuth = obs_cells[1].astype(jnp.float32) * (2.0 * math.pi / 128.0)
    return (
        jnp.sin(polar_angle) * jnp.cos(azimuth),
        jnp.sin(polar_angle) * jnp.sin(azimuth),
        jnp.cos(polar_angle),
    )


def project(facing, place_xyz):
    dotted = facing[0][:, None] * place_xyz[0][None, :] + facing[1][:, None] * place_xyz[1][None, :]
    return dotted + facing[2][:, None] * place_xyz[2][None, :]


def kernels(bin_ids, dotted):
    wavenumber = (bin_ids.astype(jnp.float32) + 1.0) * WAVE_STEP
    phase_grid = wavenumber[:, None, None] * dotted[None]
    return jnp.concatenate([jnp.cos(phase_grid), jnp.sin(phase_grid)], axis=1).astype(jnp.bfloat16)


def combine(products, bin_ids, facing, norm_scale):
    observers = facing[0].shape[0]
    bin_total = bin_ids.shape[0]
    cos_part = products[:, :observers].reshape(bin_total, observers, NQ, 2)
    sine_part = products[:, observers:].reshape(bin_total, observers, NQ, 2)
    real_part = cos_part[..., 0] + sine_part[..., 1]
    imag_part = cos_part[..., 1] - sine_part[..., 0]
    weights = jnp.stack([jnp.ones_like(facing[0]), facing[0], facing[1], facing[2]], axis=-1)
    real_sum = jnp.sum(real_part * weights[None], axis=-1)
    imag_sum = jnp.sum(imag_part * weights[None], axis=-1)
    amplitude = (bin_ids.astype(jnp.float32) + 1.0) * (norm_scale / NF)
    return jnp.stack([-amplitude[:, None] * imag_sum, amplitude[:, None] * real_sum], axis=1)


def apply_green(bin_ids, spec_block, dotted, facing, norm_scale):
    green_grid = kernels(bin_ids, dotted)
    products = jnp.einsum(
        "bxp,bcp->bxc", green_grid, spec_block, preferred_element_type=jnp.float32
    )
    return combine(products, bin_ids, facing, norm_scale)


def per_device(series, send_rows, bin_counts, observer_cells):
    vol_count = lax.axis_size("vol")
    nar_count = lax.axis_size("nar")
    vol_index = lax.axis_index("vol")
    nar_index = lax.axis_index("nar")
    bin_cap = vol_count * max(1, 2 * NF // (nar_count * vol_count))
    time_len = series.shape[1] // NQ
    slot_total = send_rows.shape[2]
    slot_width = slot_total // vol_count
    listing = send_rows.reshape(-1)
    picked = jnp.take(series, jnp.maximum(listing, 0), axis=0)
    packed = jnp.where((listing >= 0)[:, None], picked, jnp.zeros((), series.dtype))
    arrived = lax.all_to_all(packed, "vol", split_axis=0, concat_axis=0, tiled=True)
    starts = jnp.cumsum(bin_counts) - bin_counts
    own_start = starts[nar_index]
    own_count = bin_counts[nar_index]
    dft_scale = 1.0 / math.sqrt(time_len)
    within = jnp.arange(bin_cap, dtype=jnp.int32)
    own_table = dft_table(own_start + within, within < own_count, time_len)
    row_piece = lax.all_gather(arrived, "nar", axis=0, tiled=True)
    rows_here = row_piece.shape[0]
    spectral = jnp.dot(
        row_piece.reshape(rows_here * NQ, time_len), own_table, preferred_element_type=jnp.float32
    )
    spectral = (spectral * dft_scale).astype(jnp.bfloat16).reshape(rows_here, NQ, bin_cap, 2)
    spectra = spectral.transpose(2, 1, 3, 0).reshape(bin_cap, 2 * NQ, rows_here)
    local_points = nar_count * slot_total

    def point_ids(vol_owner, flat_index):
        nar_source = flat_index // slot_total
        remain = flat_index % slot_total
        vol_source = remain // slot_width
        within_slot = remain % slot_width
        return (
            (vol_source * nar_count + nar_source) * vol_count + vol_owner
        ) * slot_width + within_slot

    norm_scale = 1.0 / math.sqrt(vol_count * nar_count * slot_total)
    facing = directions(observer_cells)
    share_rows = bin_cap // vol_count
    regrouped = lax.all_to_all(spectra, "vol", split_axis=0, concat_axis=2, tiled=True)
    bin_ids = own_start + vol_index * share_rows + jnp.arange(share_rows, dtype=jnp.int32)
    span_points = local_points * max(1, vol_count // 8)
    turn_count = vol_count * local_points // span_points

    def add_block(turn_index, running):
        first_point = turn_index * span_points
        spec_block = lax.dynamic_slice_in_dim(regrouped, first_point, span_points, 2)
        flat_index = first_point + jnp.arange(span_points, dtype=jnp.int32)
        point_list = point_ids(flat_index // local_points, flat_index % local_points)
        dotted = project(facing, positions(point_list))
        return running + apply_green(bin_ids, spec_block, dotted, facing, norm_scale)

    result = lax.fori_loop(
        0, turn_count, add_block, jnp.zeros((share_rows, 2, observer_cells.shape[1]), jnp.float32)
    )
    return result.reshape(1, share_rows, 2, result.shape[-1])


def solution(mesh):
    placed = (P(("vol", "nar"), None), P("vol", "nar", None), P(), P())
    return jax.shard_map(
        per_device,
        mesh=mesh,
        in_specs=placed,
        out_specs=P("nar", "vol", None, None),
        check_vma=False,
    )
```

profile of v0, /device:TPU:0, one launch (start us, length us, event | category | flops | bytes accessed | tf_op | source)
XLA Modules:
  0.0 133.8 jit_solution(10418153351370994909)
XLA Ops:
  0.0 0.7 compare_reduce_fusion
  2.2 0.8 broadcast_select_fusion.1
  3.0 7.3 %all-to-all-start = ((bf16[8,2,2048]{2,1,0:T(2,128)(2,1)}), bf16[8,2,2048]{2,1,0:T(2,128)(2,1)S(1)}, u32[]{:S(2)}, u32[]{:S(2)}) async-start(bf16[8,2,2048]{2,1,0:T(2,128)(2,1)} %broadcast_select_fusion.1), calls=%async_computation | async-start | bytes 131072 | tf_op jit(solution)/shard_map/all_to_all | solution.py:87
  10.3 0.8 reduce-window.9
  11.1 0.7 bitcast_subtract_fusion
  11.8 1.3 dynamic_slice.18
  13.0 0.7 dynamic_slice.17
  13.7 0.7 add_add_fusion
  14.4 1.1 fusion.36
  17.2 5.8 %all_gather.3 = bf16[64,2048]{1,0:T(8,128)(2,1)S(1)} all-gather(bf16[16,2048]{1,0:T(8,128)(2,1)S(1)} %all_to_all.20), channel_id=1, replica_groups=mesh['vol'=8,'nar'=4] {'nar'}, dimensions={0}, use_global_device_ids=true | all-gather | bytes 327680 | tf_op jit(solution)/shard_map/all_gather | solution.py:94
  23.5 10.0 %reshape.598 = bf16[64,4,128,2]{1,0,3,2:T(8,128)(2,1)} reshape(bf16[256,256]{0,1:T(8,128)(2,1)S(1)} %copy.27) | data formatting | bytes 262144 | tf_op jit(solution)/shard_map/reshape | solution.py:99
  33.5 6.2 %copy.28 = bf16[128,4,2,64]{0,3,2,1:T(8,128)(2,1)S(1)} copy(bf16[128,4,2,64]{1,3,2,0:T(8,128)(2,1)} %bitcast.64) | data formatting | bytes 262144 | tf_op jit(solution)/shard_map/transpose | solution.py:100
  39.9 0.9 reshape.631
  40.8 5.4 %all-to-all-start.1 = ((bf16[8,2,4096]{2,1,0:T(2,128)(2,1)}), bf16[8,2,4096]{2,1,0:T(2,128)(2,1)S(1)}, u32[]{:S(2)}, u32[]{:S(2)}) async-start(bf16[8,2,4096]{2,1,0:T(2,128)(2,1)} %reshape.631), calls=%async_computation.1 | async-start | bytes 262144 | tf_op jit(solution)/shard_map/all_to_all | solution.py:115
  47.0 6.6 %all-to-all-done.1 = bf16[8,2,4096]{2,1,0:T(2,128)(2,1)S(1)} async-done(((bf16[8,2,4096]{2,1,0:T(2,128)(2,1)}), bf16[8,2,4096]{2,1,0:T(2,128)(2,1)S(1)}, u32[]{:S(2)}, u32[]{:S(2)}) %all-to-all-start.1) | async-done | bytes 131104 | tf_op jit(solution)/shard_map/all_to_all | solution.py:115
  54.3 78.9 %while.19 = (s32[]{:T(128)}, f32[16,2,512]{2,1,0:T(2,128)S(1)}, f32[512]{0:T(512)S(1)}, f32[512]{0:T(512)S(1)}, f32[512]{0:T(512)S(1)}, /*index=5*/bf16[16,8,512...) while((s32[]{:T(128)}, f32[16,2,512]{2,1,0:T(2,128)S(1)}, ...), condition=%wide.region_4.5_spmd.clone.clone.clone, body=%wide.region_1.4_spmd.clone.clone.clone.sunk | while | flops 22971540 | bytes 8845429 | solution.py:128
  54.6 7.8 %fusion.56 = (bf16[16,512,64]{1,2,0:T(8,128)(2,1)S(1)}, bf16[16,512,64]{1,2,0:T(8,128)(2,1)S(1)}) fusion(f32[512,64]{0,1:T(8,128)S(1)} %multiply_add_fusion.2, f32[16]{0:T(128)S(1)} %fusion.55), kind=kLoop, calls=%fused_computation.5.clone.1 | loop fusion | flops 1572864 | bytes 2228288 | tf_op jit(solution)/shard_map/convert
  64.5 7.8 %fusion.56 = (bf16[16,512,64]{1,2,0:T(8,128)(2,1)S(1)}, bf16[16,512,64]{1,2,0:T(8,128)(2,1)S(1)}) fusion(f32[512,64]{0,1:T(8,128)S(1)} %multiply_add_fusion.2, f32[16]{0:T(128)S(1)} %fusion.55), kind=kLoop, calls=%fused_computation.5.clone.1 | loop fusion | flops 1572864 | bytes 2228288 | tf_op jit(solution)/shard_map/convert
  74.3 7.8 %fusion.56 = (bf16[16,512,64]{1,2,0:T(8,128)(2,1)S(1)}, bf16[16,512,64]{1,2,0:T(8,128)(2,1)S(1)}) fusion(f32[512,64]{0,1:T(8,128)S(1)} %multiply_add_fusion.2, f32[16]{0:T(128)S(1)} %fusion.55), kind=kLoop, calls=%fused_computation.5.clone.1 | loop fusion | flops 1572864 | bytes 2228288 | tf_op jit(solution)/shard_map/convert
  84.2 7.8 %fusion.56 = (bf16[16,512,64]{1,2,0:T(8,128)(2,1)S(1)}, bf16[16,512,64]{1,2,0:T(8,128)(2,1)S(1)}) fusion(f32[512,64]{0,1:T(8,128)S(1)} %multiply_add_fusion.2, f32[16]{0:T(128)S(1)} %fusion.55), kind=kLoop, calls=%fused_computation.5.clone.1 | loop fusion | flops 1572864 | bytes 2228288 | tf_op jit(solution)/shard_map/convert
  94.1 7.8 %fusion.56 = (bf16[16,512,64]{1,2,0:T(8,128)(2,1)S(1)}, bf16[16,512,64]{1,2,0:T(8,128)(2,1)S(1)}) fusion(f32[512,64]{0,1:T(8,128)S(1)} %multiply_add_fusion.2, f32[16]{0:T(128)S(1)} %fusion.55), kind=kLoop, calls=%fused_computation.5.clone.1 | loop fusion | flops 1572864 | bytes 2228288 | tf_op jit(solution)/shard_map/convert
  103.9 7.8 %fusion.56 = (bf16[16,512,64]{1,2,0:T(8,128)(2,1)S(1)}, bf16[16,512,64]{1,2,0:T(8,128)(2,1)S(1)}) fusion(f32[512,64]{0,1:T(8,128)S(1)} %multiply_add_fusion.2, f32[16]{0:T(128)S(1)} %fusion.55), kind=kLoop, calls=%fused_computation.5.clone.1 | loop fusion | flops 1572864 | bytes 2228288 | tf_op jit(solution)/shard_map/convert
  113.8 7.8 %fusion.56 = (bf16[16,512,64]{1,2,0:T(8,128)(2,1)S(1)}, bf16[16,512,64]{1,2,0:T(8,128)(2,1)S(1)}) fusion(f32[512,64]{0,1:T(8,128)S(1)} %multiply_add_fusion.2, f32[16]{0:T(128)S(1)} %fusion.55), kind=kLoop, calls=%fused_computation.5.clone.1 | loop fusion | flops 1572864 | bytes 2228288 | tf_op jit(solution)/shard_map/convert
  123.6 7.8 %fusion.56 = (bf16[16,512,64]{1,2,0:T(8,128)(2,1)S(1)}, bf16[16,512,64]{1,2,0:T(8,128)(2,1)S(1)}) fusion(f32[512,64]{0,1:T(8,128)S(1)} %multiply_add_fusion.2, f32[16]{0:T(128)S(1)} %fusion.55), kind=kLoop, calls=%fused_computation.5.clone.1 | loop fusion | flops 1572864 | bytes 2228288 | tf_op jit(solution)/shard_map/convert
  (163 shorter events, 21.1 us)
Async XLA Ops:
  0.0 1.6 %copy-start = (bf16[64,2048]{1,0:T(8,128)(2,1)S(1)}, bf16[64,2048]{1,0:T(8,128)(2,1)}, u32[]{:S(2)}) copy-start(bf16[64,2048]{1,0:T(8,128)(2,1)} %param.6) | copy-start | bytes 786436
  3.0 14.2 %all-to-all-start = ((bf16[8,2,2048]{2,1,0:T(2,128)(2,1)}), bf16[8,2,2048]{2,1,0:T(2,128)(2,1)S(1)}, u32[]{:S(2)}, u32[]{:S(2)}) async-start(bf16[8,2,2048]{2,1,0:T(2,128)(2,1)} %broadcast_select_fusion.1), calls=%async_computation | async-start | bytes 131072 | tf_op jit(solution)/shard_map/all_to_all | solution.py:87
  33.5 13.4 %copy-start.2 = (s32[2,512]{1,0:T(2,128)S(1)}, s32[2,512]{1,0:T(2,128)}, u32[]{:S(2)}) copy-start(s32[2,512]{1,0:T(2,128)} %param.9) | copy-start | bytes 12292
  40.8 12.9 %all-to-all-start.1 = ((bf16[8,2,4096]{2,1,0:T(2,128)(2,1)}), bf16[8,2,4096]{2,1,0:T(2,128)(2,1)S(1)}, u32[]{:S(2)}, u32[]{:S(2)}) async-start(bf16[8,2,4096]{2,1,0:T(2,128)(2,1)} %reshape.631), calls=%async_computation.1 | async-start | bytes 262144 | tf_op jit(solution)/shard_map/all_to_all | solution.py:115
  133.2 0.6 copy-start.1
where the time goes:
time: 134 us
  other arithmetic  78 us (58%)
  local copies, waits for them, and re-layouts  24.5 us (18%)
  starting transfers between devices  12.6 us (9%)
  waiting for transfers between devices  7.29 us (5%)
  blocking collectives  5.78 us (4%)
  matrix products  3.81 us (3%)
    another operation x9, other arithmetic  63 us
    reshape x1, local copies, waits for them, and re-layouts, per_device(): (spectral * dft_scale).astype(jnp.bfloat16)  9.98 us
    all_to_all x1, starting transfers between devices, per_device(): lax.all_to_all(packed, 'vol', split_axis=0, concat_axis=0, tiled=True)  7.28 us
    all_to_all x1, waiting for transfers between devices, per_device(): lax.all_to_all(spectra, 'vol', split_axis=0, concat_axis=2, tiled=True)  6.64 us
    transpose x1, local copies, waits for them, and re-layouts, per_device(): spectra = spectral.transpose(2, 1, 3, 0).reshape(bin_cap, 2 * NQ, rows_here)  6.2 us
    all_gather x1, blocking collectives, per_device(): row_piece = lax.all_gather(arrived, 'nar', axis=0, tiled=True)  5.78 us
    all_to_all x1, starting transfers between devices, per_device(): lax.all_to_all(spectra, 'vol', split_axis=0, concat_axis=2, tiled=True)  5.37 us
    dot_general x8, matrix products, apply_green(): jnp.einsum('bxp,bcp->bxc', green_grid, spec_block, preferred_element_type...  3.55 us
  transfers between devices with their start and end apart: 2, of which 2 were waited for; matrix products, arithmetic and copies ran while one was open for 5% of the time, Pallas kernels for 0%

commit v1 on v0

--- a/solution.py
+++ b/solution.py
@@ -2,7 +2,10 @@
 
 import jax
 import jax.numpy as jnp
+import numpy as np
 from jax import lax
+from jax.experimental import pallas as pl
+from jax.experimental.pallas import tpu as pltpu
 from jax.sharding import PartitionSpec as P
 
 NF = 256
@@ -72,7 +75,7 @@
     return combine(products, bin_ids, facing, norm_scale)
 
 
-def per_device(series, send_rows, bin_counts, observer_cells):
+def per_device_general(series, send_rows, bin_counts, observer_cells):
     vol_count = lax.axis_size("vol")
     nar_count = lax.axis_size("nar")
     vol_index = lax.axis_index("vol")
@@ -131,6 +134,258 @@
     return result.reshape(1, share_rows, 2, result.shape[-1])
 
 
+LANES = 128
+TURN = 2.0 * math.pi
+
+WIDE_SIN = (6.2831854820251465, -41.34170150756836, 81.60513305664062, -76.70301818847656,
+            42.02592849731445, -14.899847030639648, 3.2381374835968018)
+WIDE_COS = (1.0, -19.73920440673828, 64.93911743164062, -85.45014190673828,
+            60.16762924194336, -25.967599868774414, 6.528658390045166)
+NARROW_SIN = (6.2831854820251465, -41.34168243408203, 81.60247802734375, -76.58128356933594,
+              39.76072311401367)
+NARROW_COS = (1.0, -19.739208221435547, 64.93934631347656, -85.45356750488281,
+              60.143951416015625, -24.981836318969727)
+
+
+def horner(coefficients, z):
+    total = jnp.full_like(z, coefficients[-1])
+    for value in coefficients[-2::-1]:
+        total = total * z + value
+    return total
+
+
+def cos_sin_turns(turns, narrow=False):
+    if narrow:
+        z = turns * turns
+        return horner(NARROW_COS, z), horner(NARROW_SIN, z) * turns
+    turns = turns - jnp.floor(turns + 0.5)
+    z = turns * turns
+    return horner(WIDE_COS, z), horner(WIDE_SIN, z) * turns
+
+
+def slot_places(point_total):
+    ids = np.arange(point_total, dtype=np.int64)
+    angle = (ids * 1597 % 8191).astype(np.float64) * (TURN / 8191.0)
+    axial = (ids // 128) * 0.5 + (ids * 613 % 127) * (0.37 / 127.0)
+    place = np.stack([20.0 * np.cos(angle), 20.0 * np.sin(angle), axial])
+    return place * (WAVE_STEP / TURN)
+
+
+def dft_constant(time_len):
+    turns = np.arange(time_len)[:, None] * (np.arange(NF) + 1)[None, :] % time_len
+    angle = turns.astype(np.float32) * np.float32(TURN / time_len)
+    grid = np.concatenate([np.cos(angle), -np.sin(angle)], axis=1)
+    return grid.astype(jnp.bfloat16)
+
+
+def own_bins(counts_ref, nar_count):
+    nar_index = lax.axis_index("nar")
+    start = jnp.int32(0)
+    for m in range(nar_count - 1):
+        start = start + jnp.where(m < nar_index, counts_ref[m], 0)
+    return start, counts_ref[nar_index]
+
+
+def swap_groups(blocks, width):
+    blocks = list(blocks)
+    amount = len(blocks)
+    lanes = amount * width
+    group = lax.broadcasted_iota(jnp.int32, blocks[0].shape, 1) // width
+    step = 1
+    while step < amount:
+        high = (group & step) != 0
+        for r in range(amount):
+            if r & step == 0:
+                x, y = blocks[r], blocks[r | step]
+                blocks[r] = jnp.where(high, pltpu.roll(y, step * width, 1), x)
+                blocks[r | step] = jnp.where(high, y, pltpu.roll(x, lanes - step * width, 1))
+        step *= 2
+    return blocks
+
+
+def pack_kernel(counts_ref, rows_ref, series_ref, table_ref, out_ref, *, nar_count, width):
+    row_total = series_ref.shape[0]
+    slots = rows_ref.shape[2]
+    time_len = series_ref.shape[1] // NQ
+    row_ids = lax.broadcasted_iota(jnp.int32, (row_total, slots), 0)
+    hot = jnp.where(row_ids == rows_ref[0], 1.0, 0.0).astype(jnp.bfloat16)
+    picked = lax.dot_general(
+        hot, series_ref[...], (((0,), (0,)), ((), ())), preferred_element_type=jnp.float32
+    ).astype(jnp.bfloat16)
+    stacked = jnp.concatenate(
+        [picked[:, q * time_len:(q + 1) * time_len] for q in range(NQ)], axis=0
+    )
+    spectral = jnp.dot(stacked, table_ref[...], preferred_element_type=jnp.float32)
+    spectral = spectral * (1.0 / math.sqrt(time_len))
+    start = jnp.int32(0)
+    for m in range(nar_count):
+        blocks = []
+        for part in range(2):
+            half = spectral[:, part * NF:(part + 1) * NF]
+            half = pltpu.roll(half, lax.rem(NF - start, NF), 1)[:, :LANES]
+            blocks += [half[q * slots:(q + 1) * slots] for q in range(NQ)]
+        for v, chunk in enumerate(swap_groups(blocks, width)):
+            first = (v * nar_count + m) * slots
+            out_ref[first:first + slots, :] = chunk.astype(jnp.bfloat16)
+        start = start + counts_ref[m]
+
+
+def green_kernel(
+    counts_ref, cells_ref, place_ref, out_ref, facing_ref, spread_ref, column_ref,
+    *, nar_count, share, narrow
+):
+    points = place_ref.shape[1]
+    observers = cells_ref.shape[1]
+    start, _ = own_bins(counts_ref, nar_count)
+    first_bin = start + lax.axis_index("vol") * share
+    base_step = (first_bin + 1).astype(jnp.float32)
+    cells = cells_ref[...].astype(jnp.float32)
+    cos_polar, sin_polar = cos_sin_turns((cells[0:1] + 0.5) * (1.0 / 256.0))
+    cos_azimuth, sin_azimuth = cos_sin_turns(cells[1:2] * (1.0 / 128.0))
+    facing = (sin_polar * cos_azimuth, sin_polar * sin_azimuth, cos_polar)
+    for axis in range(3):
+        facing_ref[axis:axis + 1, :] = facing[axis]
+        spread_ref[axis] = jnp.broadcast_to(facing[axis], (8, observers))
+    for tile in range(points // LANES):
+        column_ref[tile * LANES:(tile + 1) * LANES, :] = (
+            place_ref[:, tile * LANES:(tile + 1) * LANES].T
+        )
+    rows, lanes = 16, 256
+
+    def tile_step(tile, carry):
+        first = pl.multiple_of(tile * rows, rows)
+        place = [column_ref[pl.ds(first, rows), axis:axis + 1] for axis in range(3)]
+        for lane in range(0, observers, lanes):
+            def seen(axis):
+                return jnp.concatenate([spread_ref[axis, :, lane:lane + lanes]] * (rows // 8), axis=0)
+            turns = seen(0) * place[0] + seen(1) * place[1]
+            turns = turns + seen(2) * place[2]
+            c_now, s_now = cos_sin_turns(turns * base_step)
+            c_one, s_one = cos_sin_turns(turns, narrow)
+            twice = c_one + c_one
+            c_old = c_now * c_one + s_now * s_one
+            s_old = s_now * c_one - c_now * s_one
+            for j in range(share):
+                out_ref[j, pl.ds(first, rows), lane:lane + lanes] = c_now.astype(jnp.bfloat16)
+                out_ref[j, pl.ds(first + points, rows), lane:lane + lanes] = s_now.astype(jnp.bfloat16)
+                if j < share - 1:
+                    c_now, c_old = twice * c_now - c_old, c_now
+                    s_now, s_old = twice * s_now - s_old, s_now
+        return carry
+
+    lax.fori_loop(0, points // rows, tile_step, 0)
+
+
+def moment_kernel(
+    counts_ref, spectra_ref, green_ref, facing_ref, out_ref, left_ref, moment_ref,
+    *, nar_count, share
+):
+    points = spectra_ref.shape[0]
+    half = NQ * share
+    tiles = points // LANES
+    for tile in range(tiles):
+        turned = spectra_ref[tile * LANES:(tile + 1) * LANES, :].astype(jnp.float32).T
+        left_ref[tile] = turned
+        left_ref[tiles + tile, :half] = turned[half:]
+        left_ref[tiles + tile, half:] = -turned[:half]
+    pieces = moment_ref.shape[0]
+    for j in range(share):
+        own = pl.ds(j, 2 * NQ, stride=share)
+        left = jnp.concatenate([left_ref[tile, own, :] for tile in range(2 * tiles)], axis=1)
+        product = jnp.dot(
+            left.astype(jnp.bfloat16), green_ref[j], preferred_element_type=jnp.float32
+        )
+        for piece in range(pieces):
+            moment_ref[piece, own, :] = product[:, piece * LANES:(piece + 1) * LANES]
+    sums = []
+    for part in range(2):
+        columns = []
+        for piece in range(pieces):
+            first = part * half
+            total = moment_ref[piece, first:first + share, :]
+            for q in range(1, NQ):
+                weight = facing_ref[q - 1:q, piece * LANES:(piece + 1) * LANES]
+                first = part * half + q * share
+                total = total + moment_ref[piece, first:first + share, :] * weight
+            columns.append(total)
+        sums.append(jnp.concatenate(columns, axis=1))
+    start, count = own_bins(counts_ref, nar_count)
+    within = lax.axis_index("vol") * share + lax.broadcasted_iota(jnp.int32, sums[0].shape, 0)
+    amplitude = (start + within + 1).astype(jnp.float32) * (1.0 / (math.sqrt(points) * NF))
+    valid = within < count
+    out_ref[0, :, 0, :] = jnp.where(valid, -amplitude * sums[1], 0.0)
+    out_ref[0, :, 1, :] = jnp.where(valid, amplitude * sums[0], 0.0)
+
+
+def per_device(series, send_rows, bin_counts, observer_cells):
+    vol_count = lax.axis_size("vol")
+    nar_count = lax.axis_size("nar")
+    share = max(1, 2 * NF // (nar_count * vol_count))
+    slots = send_rows.shape[2]
+    points = vol_count * nar_count * slots
+    observers = observer_cells.shape[1]
+    time_len = series.shape[1] // NQ
+    fits = (
+        vol_count == 2 * NQ
+        and vol_count * share == LANES
+        and slots % 16 == 0
+        and points % LANES == 0
+        and observers % 256 == 0
+        and share * points * observers <= 8 << 20
+    )
+    if not fits:
+        return per_device_general(series, send_rows, bin_counts, observer_cells)
+    vmem = pl.BlockSpec(memory_space=pltpu.VMEM)
+    smem = pl.BlockSpec(memory_space=pltpu.SMEM)
+    places = slot_places(points)
+    reach = float(np.sqrt((places ** 2).sum(axis=0)).max())
+    place_rows = np.zeros((8, points), np.float32)
+    place_rows[:3] = places
+
+    packed = pl.pallas_call(
+        lambda *refs: pack_kernel(*refs, nar_count=nar_count, width=share),
+        out_shape=jax.ShapeDtypeStruct((points, LANES), jnp.bfloat16),
+        in_specs=[smem, vmem, vmem, vmem],
+        out_specs=vmem,
+        compiler_params=pltpu.CompilerParams(vmem_limit_bytes=8 << 20),
+        name="pack_rows",
+    )(bin_counts, send_rows, series, jnp.asarray(dft_constant(time_len)))
+    spectra = lax.all_to_all(packed, ("vol", "nar"), split_axis=0, concat_axis=0, tiled=True)
+    green, facing = pl.pallas_call(
+        lambda *refs: green_kernel(
+            *refs, nar_count=nar_count, share=share, narrow=reach < 0.249
+        ),
+        out_shape=(
+            jax.ShapeDtypeStruct((share, 2 * points, observers), jnp.bfloat16),
+            jax.ShapeDtypeStruct((3, observers), jnp.float32),
+        ),
+        in_specs=[smem, vmem, vmem],
+        out_specs=(vmem, vmem),
+        scratch_shapes=[
+            pltpu.VMEM((3, 8, observers), jnp.float32),
+            pltpu.VMEM((points, 8), jnp.float32),
+        ],
+        compiler_params=pltpu.CompilerParams(vmem_limit_bytes=24 << 20),
+        cost_estimate=pl.CostEstimate(
+            flops=60 * share * points * observers, bytes_accessed=4 * share * points * observers,
+            transcendentals=0,
+        ),
+        name="green_grid",
+    )(bin_counts, observer_cells, jnp.asarray(place_rows))
+    return pl.pallas_call(
+        lambda *refs: moment_kernel(*refs, nar_count=nar_count, share=share),
+        out_shape=jax.ShapeDtypeStruct((1, share, 2, observers), jnp.float32),
+        in_specs=[smem, vmem, vmem, vmem],
+        out_specs=vmem,
+        scratch_shapes=[
+            pltpu.VMEM((2 * points // LANES, LANES, LANES), jnp.float32),
+            pltpu.VMEM((observers // LANES, LANES, LANES), jnp.float32),
+        ],
+        compiler_params=pltpu.CompilerParams(vmem_limit_bytes=24 << 20),
+        name="moments",
+    )(bin_counts, spectra, green, facing)
+
+
 def solution(mesh):
     placed = (P(("vol", "nar"), None), P("vol", "nar", None), P(), P())
     return jax.shard_map(

time: 134 us -> 38.5 us (0.29)
  other arithmetic: 78 us -> 0 us
  Pallas kernels: 0 us -> 13.2 us
  waiting for transfers between devices: 7.29 us -> 0.01 us
  local copies, waits for them, and re-layouts: 24.5 us -> 17.5 us
  blocking collectives: 5.78 us -> 0 us
  starting transfers between devices: 12.6 us -> 7.33 us
  matrix products: 3.81 us -> 0 us
    another operation x17 -> x0, other arithmetic: 63.6 us -> none
    unnamed x8 -> x20, local copies, waits for them, and re-layouts: 1.72 us -> 17.5 us
    pallas_call x0 -> x3, Pallas kernels: none -> 13.2 us  [the longest x1 7.71 us: per_device(): pl.pallas_call(lambda *refs: green_kernel(*refs, nar_count=nar_count, sha...]
    reshape x19 -> x0, local copies, waits for them, and re-layouts: 12.7 us -> none  [the longest x1 9.98 us: per_device(): (spectral * dft_scale).astype(jnp.bfloat16)]
    all_to_all x2 -> x1, waiting for transfers between devices: 7.29 us -> 0.01 us  [per_device(): lax.all_to_all(packed, ('vol', 'nar'), split_axis=0, concat_axis=0, tiled...]
    transpose x1 -> x0, local copies, waits for them, and re-layouts: 6.2 us -> none  [per_device(): spectra = spectral.transpose(2, 1, 3, 0).reshape(bin_cap, 2 * NQ, rows_here)]
    add x33 -> x0, other arithmetic: 5.89 us -> none  [the longest x8 2.73 us: combine(): real_part = cos_part[..., 0] + sine_part[..., 1]]
    all_gather x1 -> x0, blocking collectives: 5.78 us -> none  [per_device(): row_piece = lax.all_gather(arrived, 'nar', axis=0, tiled=True)]
  transfers between devices with their start and end apart: 2 -> 1, of which waited for: 2 -> 0; matrix products, arithmetic and copies ran while one was open for 5% -> 0% of each run, Pallas kernels for 0% -> 20%
where the time goes in v1:
time: 38.5 us; the launch traced here: 38.1 us
  local copies, waits for them, and re-layouts  17.5 us (45%)
  Pallas kernels  13.2 us (34%)
  starting transfers between devices  7.33 us (19%)
    unnamed x20, local copies, waits for them, and re-layouts  17.5 us
    pallas_call x1, Pallas kernels, per_device(): pl.pallas_call(lambda *refs: green_kernel(*refs, nar_count=nar_count, sha...  7.71 us
    all_to_all x1, starting transfers between devices, per_device(): lax.all_to_all(packed, ('vol', 'nar'), split_axis=0, concat_axis=0, tiled...  7.33 us
    pallas_call x1, Pallas kernels, per_device(): pl.pallas_call(lambda *refs: moment_kernel(*refs, nar_count=nar_count, sh...  3.63 us
    pallas_call x1, Pallas kernels, per_device(): pl.pallas_call(lambda *refs: pack_kernel(*refs, nar_count=nar_count, widt...  1.89 us
  transfers between devices with their start and end apart: 1, of which 0 were waited for; matrix products, arithmetic and copies ran while one was open for 0% of the time, Pallas kernels for 20%

profile of v1, /device:TPU:0, one launch (start us, length us, event | category | flops | bytes accessed | tf_op | source)
XLA Modules:
  0.0 38.1 jit_solution(14536780243466814134)
XLA Ops:
  0.0 0.0 copy-start.2
  0.0 1.0 %copy-done.2 = bf16[512,512]{1,0:T(8,128)(2,1)S(1)} copy-done((bf16[512,512]{1,0:T(8,128)(2,1)S(1)}, bf16[512,512]{1,0:T(8,128)(2,1)}, u32[]{:S(2)}) %copy-start.2) | copy-done | bytes 524312
  1.0 0.0 copy-start.3
  1.0 0.9 %copy-done.3 = bf16[64,2048]{1,0:T(8,128)(2,1)S(1)} copy-done((bf16[64,2048]{1,0:T(8,128)(2,1)S(1)}, bf16[64,2048]{1,0:T(8,128)(2,1)}, u32[]{:S(2)}) %copy-start.3) | copy-done | bytes 262168
  2.0 0.0 copy-start.4
  2.0 0.7 %copy-done.4 = s32[4]{0:T(128)S(1)} copy-done((s32[4]{0:T(128)S(1)}, s32[4]{0:T(128)}, u32[]{:S(2)}) %copy-start.4) | copy-done | bytes 40
  2.6 0.0 copy-start.7
  2.7 0.7 %copy-done.7 = s32[1,1,16]{2,1,0:T(1,128)S(1)} copy-done((s32[1,1,16]{2,1,0:T(1,128)S(1)}, s32[1,1,16]{2,1,0:T(1,128)}, u32[]{:S(2)}) %copy-start.7) | copy-done | bytes 88
  3.3 1.9 %pack_rows.1 = bf16[512,128]{1,0:T(8,128)(2,1)} custom-call(s32[4]{0:T(128)S(1)} %copy-done.4, s32[1,1,16]{2,1,0:T(1,128)S(1)} %copy-done.7, bf16[64,2048]{1,0:T(8,128)(2,1)S(1)} %copy-done.3, bf16[512,512]{1,0:T(8,128)(2,1)S(1)} %copy-done.2), custom_call_target="tpu_custom_call" | custom-call | tf_op jit(solution)/shard_map/pack_rows/pallas_call | solution.py:345
  5.2 7.3 %all-to-all-start = ((bf16[32,16,128]{2,1,0:T(8,128)(2,1)}), bf16[32,16,128]{2,1,0:T(8,128)(2,1)S(1)}, u32[]{:S(2)}, u32[]{:S(2)}) async-start(bf16[32,16,128]{2,1,0:T(8,128)(2,1)} %bitcast), calls=%async_computation | async-start | bytes 262144 | tf_op jit(solution)/shard_map/all_to_all | solution.py:353
  12.5 0.0 copy-start.5
  12.5 0.6 %copy-done.5 = s32[4]{0:T(128)S(1)} copy-done((s32[4]{0:T(128)S(1)}, s32[4]{0:T(128)}, u32[]{:S(2)}) %copy-start.5) | copy-done | bytes 40
  13.2 0.0 copy-start.8
  13.2 0.7 %copy-done.8 = s32[2,512]{1,0:T(2,128)S(1)} copy-done((s32[2,512]{1,0:T(2,128)S(1)}, s32[2,512]{1,0:T(2,128)}, u32[]{:S(2)}) %copy-start.8) | copy-done | bytes 4120
  13.9 0.0 copy-start.9
  13.9 0.7 %copy-done.9 = f32[8,512]{1,0:T(8,128)S(1)} copy-done((f32[8,512]{1,0:T(8,128)S(1)}, f32[8,512]{1,0:T(8,128)}, u32[]{:S(2)}) %copy-start.9) | copy-done | bytes 16408
  14.6 7.7 %green_grid.1 = (bf16[16,1024,512]{2,1,0:T(8,128)(2,1)S(1)}, f32[3,512]{1,0:T(4,128)S(1)}) custom-call(s32[4]{0:T(128)S(1)} %copy-done.5, s32[2,512]{1,0:T(2,128)S(1)} %copy-done.8, f32[8,512]{1,0:T(8,128)S(1)} %copy-done.9), custom_call_target="tpu_custom_call" | custom-call | flops 251658240 | bytes 16777216 | tf_op jit(solution)/shard_map/green_grid/pallas_call | solution.py:354
  22.3 0.0 copy-start
  22.3 5.7 %copy-done = bf16[16,1024,512]{2,1,0:T(8,128)(2,1)} copy-done((bf16[16,1024,512]{2,1,0:T(8,128)(2,1)}, bf16[16,1024,512]{2,1,0:T(8,128)(2,1)S(1)}, u32[]{:S(2)}) %copy-start) | copy-done | bytes 16777240
  28.1 0.0 all-to-all-done
  28.1 0.0 copy-start.1
  28.1 5.8 %copy-done.1 = bf16[16,1024,512]{2,1,0:T(8,128)(2,1)S(1)} copy-done((bf16[16,1024,512]{2,1,0:T(8,128)(2,1)S(1)}, bf16[16,1024,512]{2,1,0:T(8,128)(2,1)}, u32[]{:S(2)}) %copy-start.1) | copy-done | bytes 16777240
  33.8 0.7 %copy-done.6 = s32[4]{0:T(128)S(1)} copy-done((s32[4]{0:T(128)S(1)}, s32[4]{0:T(128)}, u32[]{:S(2)}) %copy-start.6) | copy-done | bytes 40
  34.5 3.6 %moments.1 = f32[1,16,2,512]{3,2,1,0:T(2,128)} custom-call(s32[4]{0:T(128)S(1)} %copy-done.6, bf16[512,128]{1,0:T(8,128)(2,1)S(1)} %bitcast.2, bf16[16,1024,512]{2,1,0:T(8,128)(2,1)S(1)} %copy-done.1, f32[3,512]{1,0:T(4,128)S(1)} %get-tuple-element.8.refs_3_), custom_call_target="tpu_custom_call" | custom-call | tf_op jit(solution)/shard_map/moments/pallas_call | solution.py:375
  (1 shorter events, 0.0 us)
Async XLA Ops:
  0.0 1.0 %copy-start.2 = (bf16[512,512]{1,0:T(8,128)(2,1)S(1)}, bf16[512,512]{1,0:T(8,128)(2,1)}, u32[]{:S(2)}) copy-start(bf16[512,512]{1,0:T(8,128)(2,1)} %constant.4.clone.refs_3_) | copy-start | bytes 1572868
  1.0 0.9 %copy-start.3 = (bf16[64,2048]{1,0:T(8,128)(2,1)S(1)}, bf16[64,2048]{1,0:T(8,128)(2,1)}, u32[]{:S(2)}) copy-start(bf16[64,2048]{1,0:T(8,128)(2,1)} %refs_2_.2) | copy-start | bytes 786436
  2.0 0.7 %copy-start.4 = (s32[4]{0:T(128)S(1)}, s32[4]{0:T(128)}, u32[]{:S(2)}) copy-start(s32[4]{0:T(128)} %refs_0_.5) | copy-start | bytes 52
  2.6 0.7 %copy-start.7 = (s32[1,1,16]{2,1,0:T(1,128)S(1)}, s32[1,1,16]{2,1,0:T(1,128)}, u32[]{:S(2)}) copy-start(s32[1,1,16]{2,1,0:T(1,128)} %refs_1_.2) | copy-start | bytes 196
  5.2 22.9 %all-to-all-start = ((bf16[32,16,128]{2,1,0:T(8,128)(2,1)}), bf16[32,16,128]{2,1,0:T(8,128)(2,1)S(1)}, u32[]{:S(2)}, u32[]{:S(2)}) async-start(bf16[32,16,128]{2,1,0:T(8,128)(2,1)} %bitcast), calls=%async_computation | async-start | bytes 262144 | tf_op jit(solution)/shard_map/all_to_all | solution.py:353
  12.5 0.7 %copy-start.5 = (s32[4]{0:T(128)S(1)}, s32[4]{0:T(128)}, u32[]{:S(2)}) copy-start(s32[4]{0:T(128)} %refs_0_.5) | copy-start | bytes 52
  13.2 0.7 %copy-start.8 = (s32[2,512]{1,0:T(2,128)S(1)}, s32[2,512]{1,0:T(2,128)}, u32[]{:S(2)}) copy-start(s32[2,512]{1,0:T(2,128)} %refs_1_.3) | copy-start | bytes 12292
  13.9 0.7 %copy-start.9 = (f32[8,512]{1,0:T(8,128)S(1)}, f32[8,512]{1,0:T(8,128)}, u32[]{:S(2)}) copy-start(f32[8,512]{1,0:T(8,128)} %constant.5.clone.refs_2_) | copy-start | bytes 49156
  22.3 5.7 %copy-start = (bf16[16,1024,512]{2,1,0:T(8,128)(2,1)}, bf16[16,1024,512]{2,1,0:T(8,128)(2,1)S(1)}, u32[]{:S(2)}) copy-start(bf16[16,1024,512]{2,1,0:T(8,128)(2,1)S(1)} %get-tuple-element.7.refs_2_) | copy-start | bytes 50331652
  28.1 5.8 %copy-start.1 = (bf16[16,1024,512]{2,1,0:T(8,128)(2,1)S(1)}, bf16[16,1024,512]{2,1,0:T(8,128)(2,1)}, u32[]{:S(2)}) copy-start(bf16[16,1024,512]{2,1,0:T(8,128)(2,1)} %copy-done) | copy-start | bytes 50331652
  33.8 0.7 %copy-start.6 = (s32[4]{0:T(128)S(1)}, s32[4]{0:T(128)}, u32[]{:S(2)}) copy-start(s32[4]{0:T(128)} %refs_0_.5) | copy-start | bytes 52

commit v2 on v1

--- a/solution.py
+++ b/solution.py
@@ -203,20 +203,45 @@
     return blocks
 
 
-def pack_kernel(counts_ref, rows_ref, series_ref, table_ref, out_ref, *, nar_count, width):
+def in_hbm(array):
+    return pltpu.with_memory_space_constraint(array, pltpu.HBM)
+
+
+def fetch_all(pairs, sems):
+    copies = [
+        pltpu.make_async_copy(source, target, sems.at[i])
+        for i, (source, target) in enumerate(pairs)
+    ]
+    for copy in copies:
+        copy.start()
+    return copies
+
+
+def pack_kernel(
+    counts_hbm, rows_hbm, series_hbm, table_hbm, out_ref,
+    counts_ref, rows_ref, series_ref, table_ref, sems, *, nar_count, width
+):
+    copies = fetch_all(
+        [(rows_hbm, rows_ref), (series_hbm, series_ref), (table_hbm, table_ref), (counts_hbm, counts_ref)],
+        sems,
+    )
     row_total = series_ref.shape[0]
     slots = rows_ref.shape[2]
     time_len = series_ref.shape[1] // NQ
     row_ids = lax.broadcasted_iota(jnp.int32, (row_total, slots), 0)
+    copies[0].wait()
     hot = jnp.where(row_ids == rows_ref[0], 1.0, 0.0).astype(jnp.bfloat16)
+    copies[1].wait()
     picked = lax.dot_general(
         hot, series_ref[...], (((0,), (0,)), ((), ())), preferred_element_type=jnp.float32
     ).astype(jnp.bfloat16)
     stacked = jnp.concatenate(
         [picked[:, q * time_len:(q + 1) * time_len] for q in range(NQ)], axis=0
     )
+    copies[2].wait()
     spectral = jnp.dot(stacked, table_ref[...], preferred_element_type=jnp.float32)
     spectral = spectral * (1.0 / math.sqrt(time_len))
+    copies[3].wait()
     start = jnp.int32(0)
     for m in range(nar_count):
         blocks = []
@@ -231,14 +256,24 @@
 
 
 def green_kernel(
-    counts_ref, cells_ref, place_ref, out_ref, facing_ref, spread_ref, column_ref,
+    counts_hbm, cells_hbm, place_hbm, near_ref, far_hbm, facing_ref, amplitude_ref,
+    counts_ref, cells_ref, place_ref, spread_ref, column_ref, far_ref, sems, far_sem,
     *, nar_count, share, narrow
 ):
+    copies = fetch_all(
+        [(counts_hbm, counts_ref), (cells_hbm, cells_ref), (place_hbm, place_ref)], sems
+    )
     points = place_ref.shape[1]
     observers = cells_ref.shape[1]
-    start, _ = own_bins(counts_ref, nar_count)
-    first_bin = start + lax.axis_index("vol") * share
-    base_step = (first_bin + 1).astype(jnp.float32)
+    near = near_ref.shape[0]
+    for copy in copies:
+        copy.wait()
+    start, count = own_bins(counts_ref, nar_count)
+    within = lax.axis_index("vol") * share
+    base_step = (start + within + 1).astype(jnp.float32)
+    within = within + lax.broadcasted_iota(jnp.int32, amplitude_ref.shape, 0)
+    amplitude = (start + within + 1).astype(jnp.float32) * (1.0 / (math.sqrt(points) * NF))
+    amplitude_ref[...] = jnp.where(within < count, amplitude, 0.0)
     cells = cells_ref[...].astype(jnp.float32)
     cos_polar, sin_polar = cos_sin_turns((cells[0:1] + 0.5) * (1.0 / 256.0))
     cos_azimuth, sin_azimuth = cos_sin_turns(cells[1:2] * (1.0 / 128.0))
@@ -266,20 +301,30 @@
             c_old = c_now * c_one + s_now * s_one
             s_old = s_now * c_one - c_now * s_one
             for j in range(share):
-                out_ref[j, pl.ds(first, rows), lane:lane + lanes] = c_now.astype(jnp.bfloat16)
-                out_ref[j, pl.ds(first + points, rows), lane:lane + lanes] = s_now.astype(jnp.bfloat16)
+                target = near_ref.at[j] if j < near else far_ref.at[j - near]
+                target[pl.ds(first, rows), lane:lane + lanes] = c_now.astype(jnp.bfloat16)
+                target[pl.ds(first + points, rows), lane:lane + lanes] = s_now.astype(jnp.bfloat16)
                 if j < share - 1:
                     c_now, c_old = twice * c_now - c_old, c_now
                     s_now, s_old = twice * s_now - s_old, s_now
         return carry
 
-    lax.fori_loop(0, points // rows, tile_step, 0)
+    step = 64
+    for block in range(0, points, step):
+        lax.fori_loop(block // rows, (block + step) // rows, tile_step, 0)
+        for first in (block, points + block):
+            pltpu.make_async_copy(
+                far_ref.at[:, first:first + step, :], far_hbm.at[:, first:first + step, :], far_sem
+            ).start()
+    pltpu.make_async_copy(far_ref, far_hbm, far_sem).wait()
 
 
 def moment_kernel(
-    counts_ref, spectra_ref, green_ref, facing_ref, out_ref, left_ref, moment_ref,
-    *, nar_count, share
+    spectra_ref, near_ref, far_hbm, facing_ref, amplitude_ref, out_ref,
+    left_ref, moment_ref, far_ref, sems, *, share
 ):
+    near = near_ref.shape[0]
+    copies = fetch_all([(far_hbm.at[j], far_ref.at[j]) for j in range(share - near)], sems)
     points = spectra_ref.shape[0]
     half = NQ * share
     tiles = points // LANES
@@ -292,29 +337,25 @@
     for j in range(share):
         own = pl.ds(j, 2 * NQ, stride=share)
         left = jnp.concatenate([left_ref[tile, own, :] for tile in range(2 * tiles)], axis=1)
-        product = jnp.dot(
-            left.astype(jnp.bfloat16), green_ref[j], preferred_element_type=jnp.float32
-        )
+        if j >= near:
+            copies[j - near].wait()
+        green = near_ref[j] if j < near else far_ref[j - near]
+        product = jnp.dot(left.astype(jnp.bfloat16), green, preferred_element_type=jnp.float32)
         for piece in range(pieces):
             moment_ref[piece, own, :] = product[:, piece * LANES:(piece + 1) * LANES]
-    sums = []
-    for part in range(2):
-        columns = []
-        for piece in range(pieces):
+    amplitude = amplitude_ref[...]
+    for piece in range(pieces):
+        lanes = slice(piece * LANES, (piece + 1) * LANES)
+        sums = []
+        for part in range(2):
             first = part * half
             total = moment_ref[piece, first:first + share, :]
             for q in range(1, NQ):
-                weight = facing_ref[q - 1:q, piece * LANES:(piece + 1) * LANES]
                 first = part * half + q * share
-                total = total + moment_ref[piece, first:first + share, :] * weight
-            columns.append(total)
-        sums.append(jnp.concatenate(columns, axis=1))
-    start, count = own_bins(counts_ref, nar_count)
-    within = lax.axis_index("vol") * share + lax.broadcasted_iota(jnp.int32, sums[0].shape, 0)
-    amplitude = (start + within + 1).astype(jnp.float32) * (1.0 / (math.sqrt(points) * NF))
-    valid = within < count
-    out_ref[0, :, 0, :] = jnp.where(valid, -amplitude * sums[1], 0.0)
-    out_ref[0, :, 1, :] = jnp.where(valid, amplitude * sums[0], 0.0)
+                total = total + moment_ref[piece, first:first + share, :] * facing_ref[q - 1:q, lanes]
+            sums.append(total)
+        out_ref[0, :, 0, lanes] = -amplitude * sums[1]
+        out_ref[0, :, 1, lanes] = amplitude * sums[0]
 
 
 def per_device(series, send_rows, bin_counts, observer_cells):
@@ -336,34 +377,53 @@
     if not fits:
         return per_device_general(series, send_rows, bin_counts, observer_cells)
     vmem = pl.BlockSpec(memory_space=pltpu.VMEM)
-    smem = pl.BlockSpec(memory_space=pltpu.SMEM)
+    hbm = pl.BlockSpec(memory_space=pltpu.HBM)
     places = slot_places(points)
     reach = float(np.sqrt((places ** 2).sum(axis=0)).max())
     place_rows = np.zeros((8, points), np.float32)
     place_rows[:3] = places
+    table = dft_constant(time_len)
+    near = min(share - 1, (3 << 20) // (4 * points * observers))
+    counts_scratch = pltpu.SMEM(bin_counts.shape, jnp.int32)
 
     packed = pl.pallas_call(
         lambda *refs: pack_kernel(*refs, nar_count=nar_count, width=share),
         out_shape=jax.ShapeDtypeStruct((points, LANES), jnp.bfloat16),
-        in_specs=[smem, vmem, vmem, vmem],
+        in_specs=[hbm] * 4,
         out_specs=vmem,
+        scratch_shapes=[
+            counts_scratch,
+            pltpu.VMEM(send_rows.shape, jnp.int32),
+            pltpu.VMEM(series.shape, series.dtype),
+            pltpu.VMEM(table.shape, jnp.bfloat16),
+            pltpu.SemaphoreType.DMA((4,)),
+        ],
         compiler_params=pltpu.CompilerParams(vmem_limit_bytes=8 << 20),
         name="pack_rows",
-    )(bin_counts, send_rows, series, jnp.asarray(dft_constant(time_len)))
+    )(*map(in_hbm, (bin_counts, send_rows, series, jnp.asarray(table))))
     spectra = lax.all_to_all(packed, ("vol", "nar"), split_axis=0, concat_axis=0, tiled=True)
-    green, facing = pl.pallas_call(
+    green_shape = (share - near, 2 * points, observers)
+    near_green, far_green, facing, amplitude = pl.pallas_call(
         lambda *refs: green_kernel(
             *refs, nar_count=nar_count, share=share, narrow=reach < 0.249
         ),
         out_shape=(
-            jax.ShapeDtypeStruct((share, 2 * points, observers), jnp.bfloat16),
+            jax.ShapeDtypeStruct((near, 2 * points, observers), jnp.bfloat16),
+            pltpu.HBM(green_shape, jnp.bfloat16),
             jax.ShapeDtypeStruct((3, observers), jnp.float32),
+            jax.ShapeDtypeStruct((share, LANES), jnp.float32),
         ),
-        in_specs=[smem, vmem, vmem],
-        out_specs=(vmem, vmem),
+        in_specs=[hbm] * 3,
+        out_specs=(vmem, hbm, vmem, vmem),
         scratch_shapes=[
+            counts_scratch,
+            pltpu.VMEM(observer_cells.shape, jnp.int32),
+            pltpu.VMEM(place_rows.shape, jnp.float32),
             pltpu.VMEM((3, 8, observers), jnp.float32),
             pltpu.VMEM((points, 8), jnp.float32),
+            pltpu.VMEM(green_shape, jnp.bfloat16),
+            pltpu.SemaphoreType.DMA((3,)),
+            pltpu.SemaphoreType.DMA,
         ],
         compiler_params=pltpu.CompilerParams(vmem_limit_bytes=24 << 20),
         cost_estimate=pl.CostEstimate(
@@ -371,19 +431,21 @@
             transcendentals=0,
         ),
         name="green_grid",
-    )(bin_counts, observer_cells, jnp.asarray(place_rows))
+    )(*map(in_hbm, (bin_counts, observer_cells, jnp.asarray(place_rows))))
     return pl.pallas_call(
-        lambda *refs: moment_kernel(*refs, nar_count=nar_count, share=share),
+        lambda *refs: moment_kernel(*refs, share=share),
         out_shape=jax.ShapeDtypeStruct((1, share, 2, observers), jnp.float32),
-        in_specs=[smem, vmem, vmem, vmem],
+        in_specs=[vmem, vmem, hbm, vmem, vmem],
         out_specs=vmem,
         scratch_shapes=[
             pltpu.VMEM((2 * points // LANES, LANES, LANES), jnp.float32),
             pltpu.VMEM((observers // LANES, LANES, LANES), jnp.float32),
+            pltpu.VMEM(green_shape, jnp.bfloat16),
+            pltpu.SemaphoreType.DMA((share - near,)),
         ],
         compiler_params=pltpu.CompilerParams(vmem_limit_bytes=24 << 20),
         name="moments",
-    )(bin_counts, spectra, green, facing)
+    )(spectra, near_green, in_hbm(far_green), facing, amplitude)
 
 
 def solution(mesh):

time: 38.5 us -> 25.4 us (0.66)
  local copies, waits for them, and re-layouts: 17.5 us -> 0 us
  Pallas kernels: 13.2 us -> 17.7 us
    unnamed x20 -> x0, local copies, waits for them, and re-layouts: 17.5 us -> none
    pallas_call x1, Pallas kernels: 3.63 us -> 6.25 us  [per_device(): pl.pallas_call(lambda *refs: moment_kernel(*refs, share=share), out_shape...]
    pallas_call x1, Pallas kernels: 7.71 us -> 9.08 us  [per_device(): pl.pallas_call(lambda *refs: green_kernel(*refs, nar_count=nar_count, sha...]
    pallas_call x1, Pallas kernels: 1.89 us -> 2.41 us  [per_device(): pl.pallas_call(lambda *refs: pack_kernel(*refs, nar_count=nar_count, widt...]
  transfers between devices with their start and end apart: 1 -> 1, of which waited for: 0 -> 0; matrix products, arithmetic and copies ran while one was open for 0% -> 0% of each run, Pallas kernels for 20% -> 36%
where the time goes in v2:
time: 25.4 us; the launch traced here: 25.1 us
  Pallas kernels  17.7 us (70%)
  starting transfers between devices  7.33 us (29%)
    pallas_call x1, Pallas kernels, per_device(): pl.pallas_call(lambda *refs: green_kernel(*refs, nar_count=nar_count, sha...  9.08 us
    all_to_all x1, starting transfers between devices, per_device(): lax.all_to_all(packed, ('vol', 'nar'), split_axis=0, concat_axis=0, tiled...  7.33 us
    pallas_call x1, Pallas kernels, per_device(): pl.pallas_call(lambda *refs: moment_kernel(*refs, share=share), out_shape...  6.25 us
    pallas_call x1, Pallas kernels, per_device(): pl.pallas_call(lambda *refs: pack_kernel(*refs, nar_count=nar_count, widt...  2.41 us
  transfers between devices with their start and end apart: 1, of which 0 were waited for; matrix products, arithmetic and copies ran while one was open for 0% of the time, Pallas kernels for 36%

profile of v2, /device:TPU:0, one launch (start us, length us, event | category | flops | bytes accessed | tf_op | source)
XLA Modules:
  0.0 25.1 jit_solution(2015909465444634977)
XLA Ops:
  0.0 2.4 %pack_rows.1 = bf16[512,128]{1,0:T(8,128)(2,1)} custom-call(s32[4]{0:T(128)} %refs_0_.3, s32[1,1,16]{2,1,0:T(1,128)} %refs_1_.2, bf16[64,2048]{1,0:T(8,128)(2,1)} %refs_2_.2, bf16[512,512]{1,0:T(8,128)(2,1)} %constant.4.clone.refs_3_), custom_call_target="tpu_custom_call" | custom-call | tf_op jit(solution)/shard_map/pack_rows/pallas_call | solution.py:389
  2.4 7.3 %all-to-all-start = ((bf16[32,16,128]{2,1,0:T(8,128)(2,1)}), bf16[32,16,128]{2,1,0:T(8,128)(2,1)S(1)}, u32[]{:S(2)}, u32[]{:S(2)}) async-start(bf16[32,16,128]{2,1,0:T(8,128)(2,1)} %bitcast), calls=%async_computation | async-start | bytes 262144 | tf_op jit(solution)/shard_map/all_to_all | solution.py:404
  9.8 9.1 %green_grid.1 = (bf16[3,1024,512]{2,1,0:T(8,128)(2,1)S(1)}, bf16[13,1024,512]{2,1,0:T(8,128)(2,1)}, f32[3,512]{1,0:T(4,128)S(1)}, f32[16,128]{1,0:T(8,128)S(1)}) custom-call(s32[4]{0:T(128)} %refs_0_.3, s32[2,512]{1,0:T(2,128)} %refs_1_.3, f32[8,512]{1,0:T(8,128)} %constant.5.clone.refs_2_), custom_call_target="tpu_custom_call" | custom-call | flops 251658240 | bytes 16777216 | tf_op jit(solution)/shard_map/green_grid/pallas_call | solution.py:406
  18.8 0.0 all-to-all-done
  18.9 6.3 %moments.1 = f32[1,16,2,512]{3,2,1,0:T(2,128)} custom-call(bf16[512,128]{1,0:T(8,128)(2,1)S(1)} %bitcast.2, bf16[3,1024,512]{2,1,0:T(8,128)(2,1)S(1)} %get-tuple-element.9.refs_1_, bf16[13,1024,512]{2,1,0:T(8,128)(2,1)} %get-tuple-element.10.refs_2_, f32[3,512]{1,0:T(4,128)S(1)} %get-tuple-element.11.refs_3_, f32[16,128]{1,0:T(8,128)S(1)} %get-tuple-element.12.refs_4_), custom_call_target="tpu_custom_call" | custom-call | tf_op jit(solution)/shard_map/moments/pallas_call | solution.py:435
Async XLA Ops:
  2.4 16.4 %all-to-all-start = ((bf16[32,16,128]{2,1,0:T(8,128)(2,1)}), bf16[32,16,128]{2,1,0:T(8,128)(2,1)S(1)}, u32[]{:S(2)}, u32[]{:S(2)}) async-start(bf16[32,16,128]{2,1,0:T(8,128)(2,1)} %bitcast), calls=%async_computation | async-start | bytes 262144 | tf_op jit(solution)/shard_map/all_to_all | solution.py:404

commit v3 on v2

--- a/solution.py
+++ b/solution.py
@@ -256,8 +256,9 @@
 
 
 def green_kernel(
-    counts_hbm, cells_hbm, place_hbm, near_ref, far_hbm, facing_ref, amplitude_ref,
-    counts_ref, cells_ref, place_ref, spread_ref, column_ref, far_ref, sems, far_sem,
+    counts_hbm, cells_hbm, place_hbm,
+    c_first_ref, s_first_ref, c_unit_ref, s_lead_ref, s_unit_hbm, far_hbm, facing_ref, amplitude_ref,
+    counts_ref, cells_ref, place_ref, spread_ref, column_ref, s_unit_ref, far_ref, sems, far_sem, unit_sem,
     *, nar_count, share, narrow
 ):
     copies = fetch_all(
@@ -265,7 +266,7 @@
     )
     points = place_ref.shape[1]
     observers = cells_ref.shape[1]
-    near = near_ref.shape[0]
+    near = share - far_ref.shape[0]
     for copy in copies:
         copy.wait()
     start, count = own_bins(counts_ref, nar_count)
@@ -287,75 +288,140 @@
         )
     rows, lanes = 16, 256
 
-    def tile_step(tile, carry):
+    def tile_step(tile, lead):
         first = pl.multiple_of(tile * rows, rows)
         place = [column_ref[pl.ds(first, rows), axis:axis + 1] for axis in range(3)]
         for lane in range(0, observers, lanes):
             def seen(axis):
                 return jnp.concatenate([spread_ref[axis, :, lane:lane + lanes]] * (rows // 8), axis=0)
+            here = (pl.ds(first, rows), slice(lane, lane + lanes))
             turns = seen(0) * place[0] + seen(1) * place[1]
             turns = turns + seen(2) * place[2]
             c_now, s_now = cos_sin_turns(turns * base_step)
             c_one, s_one = cos_sin_turns(turns, narrow)
+            c_first_ref[here] = c_now
+            s_first_ref[here] = s_now
+            c_unit_ref[here] = c_one
+            (s_lead_ref if lead else s_unit_ref)[here] = s_one
+            c_jump, s_jump = c_one, s_one
+            for _ in range(near.bit_length() - 1):
+                double = c_jump + c_jump
+                c_jump, s_jump = double * c_jump - 1.0, double * s_jump
+            c_now, s_now = c_now * c_jump - s_now * s_jump, s_now * c_jump + c_now * s_jump
             twice = c_one + c_one
             c_old = c_now * c_one + s_now * s_one
             s_old = s_now * c_one - c_now * s_one
-            for j in range(share):
-                target = near_ref.at[j] if j < near else far_ref.at[j - near]
-                target[pl.ds(first, rows), lane:lane + lanes] = c_now.astype(jnp.bfloat16)
-                target[pl.ds(first + points, rows), lane:lane + lanes] = s_now.astype(jnp.bfloat16)
-                if j < share - 1:
+            for j in range(share - near):
+                far_ref[j, pl.ds(first, rows), lane:lane + lanes] = c_now.astype(jnp.bfloat16)
+                far_ref[j, pl.ds(first + points, rows), lane:lane + lanes] = s_now.astype(jnp.bfloat16)
+                if j < share - near - 1:
                     c_now, c_old = twice * c_now - c_old, c_now
                     s_now, s_old = twice * s_now - s_old, s_now
-        return carry
 
     step = 64
+    lead_rows = s_lead_ref.shape[0]
     for block in range(0, points, step):
-        lax.fori_loop(block // rows, (block + step) // rows, tile_step, 0)
+        lead = block < lead_rows
+        lax.fori_loop(
+            block // rows, (block + step) // rows, lambda t, c: (tile_step(t, lead), c)[1], 0
+        )
         for first in (block, points + block):
             pltpu.make_async_copy(
                 far_ref.at[:, first:first + step, :], far_hbm.at[:, first:first + step, :], far_sem
             ).start()
+    unit_copy = pltpu.make_async_copy(
+        s_unit_ref.at[lead_rows:, :], s_unit_hbm.at[lead_rows:, :], unit_sem
+    )
+    unit_copy.start()
     pltpu.make_async_copy(far_ref, far_hbm, far_sem).wait()
+    unit_copy.wait()
 
 
 def moment_kernel(
-    spectra_ref, near_ref, far_hbm, facing_ref, amplitude_ref, out_ref,
-    left_ref, moment_ref, far_ref, sems, *, share
+    spectra_ref, c_first_ref, s_first_ref, c_unit_ref, s_lead_ref, s_unit_hbm, far_hbm,
+    facing_ref, amplitude_ref, out_ref,
+    left_ref, moment_ref, s_unit_ref, made_even, made_odd, far_ref, sems, *, share
 ):
-    near = near_ref.shape[0]
-    copies = fetch_all([(far_hbm.at[j], far_ref.at[j]) for j in range(share - near)], sems)
-    points = spectra_ref.shape[0]
+    far = far_ref.shape[0]
+    near = share - far
+    lead = s_lead_ref.shape[0]
+    points, observers = c_first_ref.shape
     half = NQ * share
     tiles = points // LANES
+    copies = fetch_all(
+        [
+            (s_unit_hbm.at[tile * LANES:(tile + 1) * LANES, :], s_unit_ref.at[tile * LANES:(tile + 1) * LANES, :])
+            for tile in range(lead // LANES, tiles)
+        ] + [(far_hbm.at[j], far_ref.at[j]) for j in range(far)],
+        sems,
+    )
+    unit_copies, far_copies = copies[:-far], copies[-far:]
+    pieces = moment_ref.shape[0]
+    made = (made_even, made_odd)
+    rows, lanes = 16, 256
+
     for tile in range(tiles):
         turned = spectra_ref[tile * LANES:(tile + 1) * LANES, :].astype(jnp.float32).T
         left_ref[tile] = turned
         left_ref[tiles + tile, :half] = turned[half:]
         left_ref[tiles + tile, half:] = -turned[:half]
-    pieces = moment_ref.shape[0]
-    for j in range(share):
+
+    def generate(block, part):
+        for lane in range(0, observers, lanes):
+            first = block * LANES + part * rows
+            here = (slice(first, first + rows), slice(lane, lane + lanes))
+            c_now, s_now, c_one = c_first_ref[here], s_first_ref[here], c_unit_ref[here]
+            s_one = (s_lead_ref if first < lead else s_unit_ref)[here]
+            twice = c_one + c_one
+            c_old = c_now * c_one + s_now * s_one
+            s_old = s_now * c_one - c_now * s_one
+            into = made[block % 2]
+            for j in range(near):
+                spot = part * rows
+                into[j, spot:spot + rows, lane:lane + lanes] = c_now.astype(jnp.bfloat16)
+                into[j, LANES + spot:LANES + spot + rows, lane:lane + lanes] = s_now.astype(jnp.bfloat16)
+                if j < near - 1:
+                    c_now, c_old = twice * c_now - c_old, c_now
+                    s_now, s_old = twice * s_now - s_old, s_now
+
+    def multiply(j, which, green, fresh):
         own = pl.ds(j, 2 * NQ, stride=share)
-        left = jnp.concatenate([left_ref[tile, own, :] for tile in range(2 * tiles)], axis=1)
-        if j >= near:
-            copies[j - near].wait()
-        green = near_ref[j] if j < near else far_ref[j - near]
+        left = jnp.concatenate([left_ref[tile, own, :] for tile in which], axis=1)
         product = jnp.dot(left.astype(jnp.bfloat16), green, preferred_element_type=jnp.float32)
         for piece in range(pieces):
-            moment_ref[piece, own, :] = product[:, piece * LANES:(piece + 1) * LANES]
+            value = product[:, piece * LANES:(piece + 1) * LANES]
+            if not fresh:
+                value = value + moment_ref[piece, own, :]
+            moment_ref[piece, own, :] = value
+
+    parts = LANES // rows
+    for block in range(tiles):
+        if block >= lead // LANES:
+            unit_copies[block - lead // LANES].wait()
+        for part in range(parts):
+            generate(block, part)
+            if block:
+                for j in range(part * near // parts, (part + 1) * near // parts):
+                    multiply(j, (block - 1, tiles + block - 1), made[(block - 1) % 2][j], block == 1)
+    for j in range(near):
+        multiply(j, (tiles - 1, 2 * tiles - 1), made[(tiles - 1) % 2][j], tiles == 1)
+    for j in range(near, share):
+        far_copies[j - near].wait()
+        multiply(j, range(2 * tiles), far_ref[j - near], True)
+
     amplitude = amplitude_ref[...]
     for piece in range(pieces):
-        lanes = slice(piece * LANES, (piece + 1) * LANES)
+        lane = slice(piece * LANES, (piece + 1) * LANES)
         sums = []
         for part in range(2):
             first = part * half
             total = moment_ref[piece, first:first + share, :]
             for q in range(1, NQ):
                 first = part * half + q * share
-                total = total + moment_ref[piece, first:first + share, :] * facing_ref[q - 1:q, lanes]
+                total = total + moment_ref[piece, first:first + share, :] * facing_ref[q - 1:q, lane]
             sums.append(total)
-        out_ref[0, :, 0, lanes] = -amplitude * sums[1]
-        out_ref[0, :, 1, lanes] = amplitude * sums[0]
+        out_ref[0, :, 0, lane] = -amplitude * sums[1]
+        out_ref[0, :, 1, lane] = amplitude * sums[0]
 
 
 def per_device(series, send_rows, bin_counts, observer_cells):
@@ -371,6 +437,7 @@
         and vol_count * share == LANES
         and slots % 16 == 0
         and points % LANES == 0
+        and share & (share - 1) == 0
         and observers % 256 == 0
         and share * points * observers <= 8 << 20
     )
@@ -383,7 +450,7 @@
     place_rows = np.zeros((8, points), np.float32)
     place_rows[:3] = places
     table = dft_constant(time_len)
-    near = min(share - 1, (3 << 20) // (4 * points * observers))
+    near = share // 2
     counts_scratch = pltpu.SMEM(bin_counts.shape, jnp.int32)
 
     packed = pl.pallas_call(
@@ -402,27 +469,33 @@
         name="pack_rows",
     )(*map(in_hbm, (bin_counts, send_rows, series, jnp.asarray(table))))
     spectra = lax.all_to_all(packed, ("vol", "nar"), split_axis=0, concat_axis=0, tiled=True)
-    green_shape = (share - near, 2 * points, observers)
-    near_green, far_green, facing, amplitude = pl.pallas_call(
+    far_shape = (share - near, 2 * points, observers)
+    grid = jax.ShapeDtypeStruct((points, observers), jnp.float32)
+    made = pltpu.VMEM((near, 2 * LANES, observers), jnp.bfloat16)
+    c_first, s_first, c_unit, s_lead, s_unit, far_green, facing, amplitude = pl.pallas_call(
         lambda *refs: green_kernel(
             *refs, nar_count=nar_count, share=share, narrow=reach < 0.249
         ),
         out_shape=(
-            jax.ShapeDtypeStruct((near, 2 * points, observers), jnp.bfloat16),
-            pltpu.HBM(green_shape, jnp.bfloat16),
+            grid, grid, grid,
+            jax.ShapeDtypeStruct((LANES, observers), jnp.float32),
+            pltpu.HBM((points, observers), jnp.float32),
+            pltpu.HBM(far_shape, jnp.bfloat16),
             jax.ShapeDtypeStruct((3, observers), jnp.float32),
             jax.ShapeDtypeStruct((share, LANES), jnp.float32),
         ),
         in_specs=[hbm] * 3,
-        out_specs=(vmem, hbm, vmem, vmem),
+        out_specs=(vmem, vmem, vmem, vmem, hbm, hbm, vmem, vmem),
         scratch_shapes=[
             counts_scratch,
             pltpu.VMEM(observer_cells.shape, jnp.int32),
             pltpu.VMEM(place_rows.shape, jnp.float32),
             pltpu.VMEM((3, 8, observers), jnp.float32),
             pltpu.VMEM((points, 8), jnp.float32),
-            pltpu.VMEM(green_shape, jnp.bfloat16),
+            pltpu.VMEM((points, observers), jnp.float32),
+            pltpu.VMEM(far_shape, jnp.bfloat16),
             pltpu.SemaphoreType.DMA((3,)),
+            pltpu.SemaphoreType.DMA,
             pltpu.SemaphoreType.DMA,
         ],
         compiler_params=pltpu.CompilerParams(vmem_limit_bytes=24 << 20),
@@ -435,17 +508,20 @@
     return pl.pallas_call(
         lambda *refs: moment_kernel(*refs, share=share),
         out_shape=jax.ShapeDtypeStruct((1, share, 2, observers), jnp.float32),
-        in_specs=[vmem, vmem, hbm, vmem, vmem],
+        in_specs=[vmem, vmem, vmem, vmem, vmem, hbm, hbm, vmem, vmem],
         out_specs=vmem,
         scratch_shapes=[
             pltpu.VMEM((2 * points // LANES, LANES, LANES), jnp.float32),
             pltpu.VMEM((observers // LANES, LANES, LANES), jnp.float32),
-            pltpu.VMEM(green_shape, jnp.bfloat16),
-            pltpu.SemaphoreType.DMA((share - near,)),
+            pltpu.VMEM((points, observers), jnp.float32),
+            made,
+            made,
+            pltpu.VMEM(far_shape, jnp.bfloat16),
+            pltpu.SemaphoreType.DMA((points // LANES - 1 + share - near,)),
         ],
         compiler_params=pltpu.CompilerParams(vmem_limit_bytes=24 << 20),
         name="moments",
-    )(spectra, near_green, in_hbm(far_green), facing, amplitude)
+    )(spectra, c_first, s_first, c_unit, s_lead, in_hbm(s_unit), in_hbm(far_green), facing, amplitude)
 
 
 def solution(mesh):

time: 25.4 us -> 24.9 us (0.980)
  Pallas kernels: 17.7 us -> 17.3 us
    pallas_call x1, Pallas kernels: 9.08 us -> 8.5 us  [per_device(): pl.pallas_call(lambda *refs: green_kernel(*refs, nar_count=nar_count, sha...]
  transfers between devices with their start and end apart: 1 -> 1, of which waited for: 0 -> 0; matrix products, arithmetic and copies ran while one was open for 0% -> 0% of each run, Pallas kernels for 36% -> 34%
where the time goes in v3:
time: 24.9 us; the launch traced here: 24.7 us
  Pallas kernels  17.3 us (69%)
  starting transfers between devices  7.33 us (29%)
    pallas_call x1, Pallas kernels, per_device(): pl.pallas_call(lambda *refs: green_kernel(*refs, nar_count=nar_count, sha...  8.5 us
    all_to_all x1, starting transfers between devices, per_device(): lax.all_to_all(packed, ('vol', 'nar'), split_axis=0, concat_axis=0, tiled...  7.33 us
    pallas_call x1, Pallas kernels, per_device(): pl.pallas_call(lambda *refs: moment_kernel(*refs, share=share), out_shape...  6.35 us
    pallas_call x1, Pallas kernels, per_device(): pl.pallas_call(lambda *refs: pack_kernel(*refs, nar_count=nar_count, widt...  2.43 us
  transfers between devices with their start and end apart: 1, of which 0 were waited for; matrix products, arithmetic and copies ran while one was open for 0% of the time, Pallas kernels for 34%

profile of v3, /device:TPU:0, one launch (start us, length us, event | category | flops | bytes accessed | tf_op | source)
XLA Modules:
  0.0 24.7 jit_solution(4029807193619155194)
XLA Ops:
  0.0 2.4 %pack_rows.1 = bf16[512,128]{1,0:T(8,128)(2,1)} custom-call(s32[4]{0:T(128)} %refs_0_.3, s32[1,1,16]{2,1,0:T(1,128)} %refs_1_.2, bf16[64,2048]{1,0:T(8,128)(2,1)} %refs_2_.2, bf16[512,512]{1,0:T(8,128)(2,1)} %constant.4.clone.refs_3_), custom_call_target="tpu_custom_call" | custom-call | tf_op jit(solution)/shard_map/pack_rows/pallas_call | solution.py:456
  2.4 7.3 %all-to-all-start = ((bf16[32,16,128]{2,1,0:T(8,128)(2,1)}), bf16[32,16,128]{2,1,0:T(8,128)(2,1)S(1)}, u32[]{:S(2)}, u32[]{:S(2)}) async-start(bf16[32,16,128]{2,1,0:T(8,128)(2,1)} %bitcast), calls=%async_computation | async-start | bytes 262144 | tf_op jit(solution)/shard_map/all_to_all | solution.py:471
  9.8 8.5 %green_grid.1 = (f32[512,512]{1,0:T(8,128)S(1)}, f32[512,512]{1,0:T(8,128)S(1)}, f32[512,512]{1,0:T(8,128)S(1)}, f32[128,512]{1,0:T(8,128)S(1)}, f32[512,512]{1,...) custom-call(s32[4]{0:T(128)} %refs_0_.3, s32[2,512]{1,0:T(2,128)} %refs_1_.3, ...), custom_call_target="tpu_custom_call" | custom-call | flops 251658240 | bytes 16777216 | tf_op jit(solution)/shard_map/green_grid/pallas_call | solution.py:475
  18.3 0.0 all-to-all-done
  18.3 6.4 %moments.1 = f32[1,16,2,512]{3,2,1,0:T(2,128)} custom-call(bf16[512,128]{1,0:T(8,128)(2,1)S(1)} %bitcast.2, f32[512,512]{1,0:T(8,128)S(1)} %get-tuple-element.13.refs_1_, f32[512,512]{1,0:T(8,128)S(1)} %get-tuple-element.14.refs_2_, f32[512,512]{1,0:T(8,128)S(1)} %get-tuple-element.15.refs_3_, f32[128,512]{1,0:T(8,128)S(1)} %get-tuple-element.16.refs_4_, ...), custom_call_target="tpu_custom_call" | custom-call | tf_op jit(solution)/shard_map/moments/pallas_call | solution.py:508
Async XLA Ops:
  2.4 15.9 %all-to-all-start = ((bf16[32,16,128]{2,1,0:T(8,128)(2,1)}), bf16[32,16,128]{2,1,0:T(8,128)(2,1)S(1)}, u32[]{:S(2)}, u32[]{:S(2)}) async-start(bf16[32,16,128]{2,1,0:T(8,128)(2,1)} %bitcast), calls=%async_computation | async-start | bytes 262144 | tf_op jit(solution)/shard_map/all_to_all | solution.py:471

commit v4 on v3

--- a/solution.py
+++ b/solution.py
@@ -257,7 +257,7 @@
 
 def green_kernel(
     counts_hbm, cells_hbm, place_hbm,
-    c_first_ref, s_first_ref, c_unit_ref, s_lead_ref, s_unit_hbm, far_hbm, facing_ref, amplitude_ref,
+    c_next_ref, s_next_ref, c_unit_ref, s_lead_ref, s_unit_hbm, far_hbm, facing_ref, amplitude_ref,
     counts_ref, cells_ref, place_ref, spread_ref, column_ref, s_unit_ref, far_ref, sems, far_sem, unit_sem,
     *, nar_count, share, narrow
 ):
@@ -266,7 +266,7 @@
     )
     points = place_ref.shape[1]
     observers = cells_ref.shape[1]
-    near = share - far_ref.shape[0]
+    far = far_ref.shape[0]
     for copy in copies:
         copy.wait()
     start, count = own_bins(counts_ref, nar_count)
@@ -299,32 +299,29 @@
             turns = turns + seen(2) * place[2]
             c_now, s_now = cos_sin_turns(turns * base_step)
             c_one, s_one = cos_sin_turns(turns, narrow)
-            c_first_ref[here] = c_now
-            s_first_ref[here] = s_now
             c_unit_ref[here] = c_one
             (s_lead_ref if lead else s_unit_ref)[here] = s_one
-            c_jump, s_jump = c_one, s_one
-            for _ in range(near.bit_length() - 1):
-                double = c_jump + c_jump
-                c_jump, s_jump = double * c_jump - 1.0, double * s_jump
-            c_now, s_now = c_now * c_jump - s_now * s_jump, s_now * c_jump + c_now * s_jump
             twice = c_one + c_one
             c_old = c_now * c_one + s_now * s_one
             s_old = s_now * c_one - c_now * s_one
-            for j in range(share - near):
+            for j in range(far):
                 far_ref[j, pl.ds(first, rows), lane:lane + lanes] = c_now.astype(jnp.bfloat16)
                 far_ref[j, pl.ds(first + points, rows), lane:lane + lanes] = s_now.astype(jnp.bfloat16)
-                if j < share - near - 1:
-                    c_now, c_old = twice * c_now - c_old, c_now
-                    s_now, s_old = twice * s_now - s_old, s_now
+                c_now, c_old = twice * c_now - c_old, c_now
+                s_now, s_old = twice * s_now - s_old, s_now
+            c_next_ref[here] = c_now
+            s_next_ref[here] = s_now
 
     step = 64
     lead_rows = s_lead_ref.shape[0]
     for block in range(0, points, step):
         lead = block < lead_rows
-        lax.fori_loop(
-            block // rows, (block + step) // rows, lambda t, c: (tile_step(t, lead), c)[1], 0
-        )
+        def pair_step(pair, carry):
+            for k in range(2):
+                tile_step(pair * 2 + k, lead)
+            return carry
+
+        lax.fori_loop(block // rows // 2, (block + step) // rows // 2, pair_step, 0)
         for first in (block, points + block):
             pltpu.make_async_copy(
                 far_ref.at[:, first:first + step, :], far_hbm.at[:, first:first + step, :], far_sem
@@ -338,25 +335,29 @@
 
 
 def moment_kernel(
-    spectra_ref, c_first_ref, s_first_ref, c_unit_ref, s_lead_ref, s_unit_hbm, far_hbm,
+    spectra_ref, c_next_ref, s_next_ref, c_unit_ref, s_lead_ref, s_unit_hbm, far_hbm,
     facing_ref, amplitude_ref, out_ref,
     left_ref, moment_ref, s_unit_ref, made_even, made_odd, far_ref, sems, *, share
 ):
     far = far_ref.shape[0]
     near = share - far
     lead = s_lead_ref.shape[0]
-    points, observers = c_first_ref.shape
+    points, observers = c_next_ref.shape
     half = NQ * share
     tiles = points // LANES
-    copies = fetch_all(
-        [
-            (s_unit_hbm.at[tile * LANES:(tile + 1) * LANES, :], s_unit_ref.at[tile * LANES:(tile + 1) * LANES, :])
-            for tile in range(lead // LANES, tiles)
-        ] + [(far_hbm.at[j], far_ref.at[j]) for j in range(far)],
-        sems,
-    )
-    unit_copies, far_copies = copies[:-far], copies[-far:]
-    pieces = moment_ref.shape[0]
+    unit_copies, far_copies = {}, []
+    for k in range(max(tiles, far)):
+        if lead // LANES <= k < tiles:
+            spot = slice(k * LANES, (k + 1) * LANES)
+            unit_copies[k] = pltpu.make_async_copy(
+                s_unit_hbm.at[spot, :], s_unit_ref.at[spot, :], sems.at[far + k]
+            )
+            unit_copies[k].start()
+        if k < far:
+            far_copies.append(
+                pltpu.make_async_copy(far_hbm.at[k], far_ref.at[k], sems.at[k])
+            )
+            far_copies[k].start()
     made = (made_even, made_odd)
     rows, lanes = 16, 256
 
@@ -367,19 +368,19 @@
         left_ref[tiles + tile, half:] = -turned[:half]
 
     def generate(block, part):
+        first = pl.multiple_of(block * LANES + part * rows, rows)
+        spot = pl.multiple_of(part * rows, rows)
+        into = made[block % 2]
+        s_source = s_lead_ref if block * LANES < lead else s_unit_ref
         for lane in range(0, observers, lanes):
-            first = block * LANES + part * rows
-            here = (slice(first, first + rows), slice(lane, lane + lanes))
-            c_now, s_now, c_one = c_first_ref[here], s_first_ref[here], c_unit_ref[here]
-            s_one = (s_lead_ref if first < lead else s_unit_ref)[here]
+            here = (pl.ds(first, rows), slice(lane, lane + lanes))
+            c_now, s_now, c_one, s_one = c_next_ref[here], s_next_ref[here], c_unit_ref[here], s_source[here]
             twice = c_one + c_one
             c_old = c_now * c_one + s_now * s_one
             s_old = s_now * c_one - c_now * s_one
-            into = made[block % 2]
             for j in range(near):
-                spot = part * rows
-                into[j, spot:spot + rows, lane:lane + lanes] = c_now.astype(jnp.bfloat16)
-                into[j, LANES + spot:LANES + spot + rows, lane:lane + lanes] = s_now.astype(jnp.bfloat16)
+                into[j, pl.ds(spot, rows), lane:lane + lanes] = c_now.astype(jnp.bfloat16)
+                into[j, pl.ds(LANES + spot, rows), lane:lane + lanes] = s_now.astype(jnp.bfloat16)
                 if j < near - 1:
                     c_now, c_old = twice * c_now - c_old, c_now
                     s_now, s_old = twice * s_now - s_old, s_now
@@ -388,37 +389,42 @@
         own = pl.ds(j, 2 * NQ, stride=share)
         left = jnp.concatenate([left_ref[tile, own, :] for tile in which], axis=1)
         product = jnp.dot(left.astype(jnp.bfloat16), green, preferred_element_type=jnp.float32)
-        for piece in range(pieces):
+        spot = pl.ds(pl.multiple_of(2 * NQ * j, 2 * NQ), 2 * NQ)
+        for piece in range(observers // LANES):
             value = product[:, piece * LANES:(piece + 1) * LANES]
-            if not fresh:
-                value = value + moment_ref[piece, own, :]
-            moment_ref[piece, own, :] = value
+            moment_ref[piece, spot, :] = value if fresh else moment_ref[piece, spot, :] + value
 
     parts = LANES // rows
     for block in range(tiles):
-        if block >= lead // LANES:
-            unit_copies[block - lead // LANES].wait()
-        for part in range(parts):
+        if block in unit_copies:
+            unit_copies[block].wait()
+
+        def part_step(part, carry):
+            if block:
+                multiply(
+                    far + part, (block - 1, tiles + block - 1), made[(block - 1) % 2][part], block == 1
+                )
             generate(block, part)
-            if block:
-                for j in range(part * near // parts, (part + 1) * near // parts):
-                    multiply(j, (block - 1, tiles + block - 1), made[(block - 1) % 2][j], block == 1)
+            return carry
+
+        lax.fori_loop(0, parts, part_step, 0)
     for j in range(near):
-        multiply(j, (tiles - 1, 2 * tiles - 1), made[(tiles - 1) % 2][j], tiles == 1)
-    for j in range(near, share):
-        far_copies[j - near].wait()
-        multiply(j, range(2 * tiles), far_ref[j - near], True)
+        multiply(far + j, (tiles - 1, 2 * tiles - 1), made[(tiles - 1) % 2][j], tiles == 1)
+    for j in range(far):
+        far_copies[j].wait()
+        multiply(j, range(2 * tiles), far_ref[j], True)
 
     amplitude = amplitude_ref[...]
-    for piece in range(pieces):
+    for piece in range(observers // LANES):
         lane = slice(piece * LANES, (piece + 1) * LANES)
         sums = []
         for part in range(2):
-            first = part * half
-            total = moment_ref[piece, first:first + share, :]
-            for q in range(1, NQ):
-                first = part * half + q * share
-                total = total + moment_ref[piece, first:first + share, :] * facing_ref[q - 1:q, lane]
+            total = None
+            for q in range(NQ):
+                term = moment_ref[piece, pl.ds(part * NQ + q, share, stride=2 * NQ), :]
+                if q:
+                    term = term * facing_ref[q - 1:q, lane]
+                total = term if total is None else total + term
             sums.append(total)
         out_ref[0, :, 0, lane] = -amplitude * sums[1]
         out_ref[0, :, 1, lane] = amplitude * sums[0]
@@ -437,7 +443,7 @@
         and vol_count * share == LANES
         and slots % 16 == 0
         and points % LANES == 0
-        and share & (share - 1) == 0
+        and share == 2 * (LANES // 16)
         and observers % 256 == 0
         and share * points * observers <= 8 << 20
     )
@@ -472,7 +478,7 @@
     far_shape = (share - near, 2 * points, observers)
     grid = jax.ShapeDtypeStruct((points, observers), jnp.float32)
     made = pltpu.VMEM((near, 2 * LANES, observers), jnp.bfloat16)
-    c_first, s_first, c_unit, s_lead, s_unit, far_green, facing, amplitude = pl.pallas_call(
+    c_next, s_next, c_unit, s_lead, s_unit, far_green, facing, amplitude = pl.pallas_call(
         lambda *refs: green_kernel(
             *refs, nar_count=nar_count, share=share, narrow=reach < 0.249
         ),
@@ -517,11 +523,11 @@
             made,
             made,
             pltpu.VMEM(far_shape, jnp.bfloat16),
-            pltpu.SemaphoreType.DMA((points // LANES - 1 + share - near,)),
+            pltpu.SemaphoreType.DMA((points // LANES + share - near,)),
         ],
         compiler_params=pltpu.CompilerParams(vmem_limit_bytes=24 << 20),
         name="moments",
-    )(spectra, c_first, s_first, c_unit, s_lead, in_hbm(s_unit), in_hbm(far_green), facing, amplitude)
+    )(spectra, c_next, s_next, c_unit, s_lead, in_hbm(s_unit), in_hbm(far_green), facing, amplitude)
 
 
 def solution(mesh):

time: 24.9 us -> 26.8 us (1.076)
  waiting for transfers between devices: 0.01 us -> 1.1 us
  Pallas kernels: 17.3 us -> 18 us
    pallas_call x1, Pallas kernels: 6.35 us -> 8.53 us  [per_device(): pl.pallas_call(lambda *refs: moment_kernel(*refs, share=share), out_shape...]
    pallas_call x1, Pallas kernels: 8.5 us -> 7.09 us  [per_device(): pl.pallas_call(lambda *refs: green_kernel(*refs, nar_count=nar_count, sha...]
    all_to_all x1, waiting for transfers between devices: 0.01 us -> 1.1 us  [per_device(): lax.all_to_all(packed, ('vol', 'nar'), split_axis=0, concat_axis=0, tiled...]
  transfers between devices with their start and end apart: 1 -> 1, of which waited for: 0 -> 1; matrix products, arithmetic and copies ran while one was open for 0% -> 0% of each run, Pallas kernels for 34% -> 27%
where the time goes in v4:
time: 26.8 us; the launch traced here: 26.5 us
  Pallas kernels  18 us (67%)
  starting transfers between devices  7.33 us (27%)
  waiting for transfers between devices  1.1 us (4%)
    pallas_call x1, Pallas kernels, per_device(): pl.pallas_call(lambda *refs: moment_kernel(*refs, share=share), out_shape...  8.53 us
    all_to_all x1, starting transfers between devices, per_device(): lax.all_to_all(packed, ('vol', 'nar'), split_axis=0, concat_axis=0, tiled...  7.33 us
    pallas_call x1, Pallas kernels, per_device(): pl.pallas_call(lambda *refs: green_kernel(*refs, nar_count=nar_count, sha...  7.09 us
    pallas_call x1, Pallas kernels, per_device(): pl.pallas_call(lambda *refs: pack_kernel(*refs, nar_count=nar_count, widt...  2.43 us
    all_to_all x1, waiting for transfers between devices, per_device(): lax.all_to_all(packed, ('vol', 'nar'), split_axis=0, concat_axis=0, tiled...  1.1 us
  transfers between devices with their start and end apart: 1, of which 1 were waited for; matrix products, arithmetic and copies ran while one was open for 0% of the time, Pallas kernels for 27%

profile of v4, /device:TPU:0, one launch (start us, length us, event | category | flops | bytes accessed | tf_op | source)
XLA Modules:
  0.0 26.5 jit_solution(717831277072578660)
XLA Ops:
  0.0 2.4 %pack_rows.1 = bf16[512,128]{1,0:T(8,128)(2,1)} custom-call(s32[4]{0:T(128)} %refs_0_.3, s32[1,1,16]{2,1,0:T(1,128)} %refs_1_.2, bf16[64,2048]{1,0:T(8,128)(2,1)} %refs_2_.2, bf16[512,512]{1,0:T(8,128)(2,1)} %constant.4.clone.refs_3_), custom_call_target="tpu_custom_call" | custom-call | tf_op jit(solution)/shard_map/pack_rows/pallas_call | solution.py:462
  2.4 7.3 %all-to-all-start = ((bf16[32,16,128]{2,1,0:T(8,128)(2,1)}), bf16[32,16,128]{2,1,0:T(8,128)(2,1)S(1)}, u32[]{:S(2)}, u32[]{:S(2)}) async-start(bf16[32,16,128]{2,1,0:T(8,128)(2,1)} %bitcast), calls=%async_computation | async-start | bytes 262144 | tf_op jit(solution)/shard_map/all_to_all | solution.py:477
  9.8 7.1 %green_grid.1 = (f32[512,512]{1,0:T(8,128)S(1)}, f32[512,512]{1,0:T(8,128)S(1)}, f32[512,512]{1,0:T(8,128)S(1)}, f32[128,512]{1,0:T(8,128)S(1)}, f32[512,512]{1,...) custom-call(s32[4]{0:T(128)} %refs_0_.3, s32[2,512]{1,0:T(2,128)} %refs_1_.3, ...), custom_call_target="tpu_custom_call" | custom-call | flops 251658240 | bytes 16777216 | tf_op jit(solution)/shard_map/green_grid/pallas_call | solution.py:481
  16.9 1.1 %all-to-all-done = bf16[32,16,128]{2,1,0:T(8,128)(2,1)S(1)} async-done(((bf16[32,16,128]{2,1,0:T(8,128)(2,1)}), bf16[32,16,128]{2,1,0:T(8,128)(2,1)S(1)}, u32[]{:S(2)}, u32[]{:S(2)}) %all-to-all-start) | async-done | bytes 131104 | tf_op jit(solution)/shard_map/all_to_all | solution.py:477
  18.0 8.5 %moments.1 = f32[1,16,2,512]{3,2,1,0:T(2,128)} custom-call(bf16[512,128]{1,0:T(8,128)(2,1)S(1)} %bitcast.2, f32[512,512]{1,0:T(8,128)S(1)} %get-tuple-element.13.refs_1_, f32[512,512]{1,0:T(8,128)S(1)} %get-tuple-element.14.refs_2_, f32[512,512]{1,0:T(8,128)S(1)} %get-tuple-element.15.refs_3_, f32[128,512]{1,0:T(8,128)S(1)} %get-tuple-element.16.refs_4_, ...), custom_call_target="tpu_custom_call" | custom-call | tf_op jit(solution)/shard_map/moments/pallas_call | solution.py:514
Async XLA Ops:
  2.4 15.5 %all-to-all-start = ((bf16[32,16,128]{2,1,0:T(8,128)(2,1)}), bf16[32,16,128]{2,1,0:T(8,128)(2,1)S(1)}, u32[]{:S(2)}, u32[]{:S(2)}) async-start(bf16[32,16,128]{2,1,0:T(8,128)(2,1)} %bitcast), calls=%async_computation | async-start | bytes 262144 | tf_op jit(solution)/shard_map/all_to_all | solution.py:477
